TPU v7x, 256 devices: a whole 4x4x8 slice. The times are simulated.
256 devices in a mesh: ctx: 16 (over z, core), tp: 16 (over y, x).
Axes of the slice: x: 4, y: 4, z: 8, core: 2. Of those that a mesh axis runs over, the one named last changes fastest.
Arguments:
- queries: bfloat16 [32768, 4096], P(('ctx', 'tp')), may hold values from -6 to 6, as said below
- keys: bfloat16 [32768, 2048], P(('ctx', 'tp')), may hold values from -9 to 9, as said below
- values: bfloat16 [32768, 2048], P(('ctx', 'tp')), may hold values from -5 to 5
- output_gradient: bfloat16 [32768, 4096], P(('ctx', 'tp')), may hold values from -5 to 5
Outputs:
- attn_out: bfloat16 [32768, 4096], P(('ctx', 'tp'))
- grad_q: bfloat16 [32768, 4096], P(('ctx', 'tp'))
- grad_k: bfloat16 [32768, 2048], P(('ctx', 'tp'))
- grad_v: bfloat16 [32768, 2048], P(('ctx', 'tp'))
Inputs may be any that keep to these rules, and one draw needn't show every extreme that they name: queries are real-valued. keys are real-valued.
All inputs are finite; a program needn't handle non-finite values.
Results may differ from a plain program's by a relative error of at most 0.023.
Values may be sent and summed in bfloat16 or wider, within the bound.
A program may use at most 128 MiB of HBM per device.

v0:
```python
import functools
import math

import jax
import jax.numpy as jnp
from jax import lax
from jax.experimental import pallas as pl
from jax.experimental.pallas import tpu as pltpu
from jax.sharding import PartitionSpec as P

HEAD = 128
GROUP = 2
WINDOW = 1024
QSCALE = 168
SCALE = QSCALE ** (-0.5)
EXP_SCALE = SCALE * math.log2(math.e)
FAR = 1e30
MESH = pl.DeviceIdType.MESH
F32 = jnp.float32
BF16 = jnp.bfloat16


def attention_kernel(
    tp, ctx, rows,
    q_in, k_in, v_in, g_in,
    o_out, dq_out, dk_out, dv_out,
    qs, kx, vx, gs, kt, vt, scores, ex, ot, rl, acc_k, acc_v, dlog,
    o_buf, dq_buf, dk_buf, dv_buf, halo_out, halo_in,
    in_send, in_recv, out_send, out_recv, halo_send, halo_recv, own_in, own_out,
):
    me = lax.axis_index("tp")
    place = lax.axis_index("ctx")
    ahead, behind = lax.rem(place + 1, ctx), lax.rem(place + ctx - 1, ctx)
    shard = rows * tp
    blocks = shard // rows
    span = WINDOW + rows
    halo_blocks = WINDOW // rows
    wide = GROUP * HEAD

    def at(i, size=rows):
        return pl.ds(pl.multiple_of(i * rows, rows), size)

    def columns(i, width):
        return pl.ds(pl.multiple_of(i * width, width), width)

    barrier = pltpu.get_barrier_semaphore()
    for n in range(1, tp):
        pl.semaphore_signal(barrier, inc=1, device_id={"tp": lax.rem(me + n, tp)}, device_id_type=MESH)
    pl.semaphore_signal(barrier, inc=1, device_id={"ctx": ahead}, device_id_type=MESH)
    pl.semaphore_signal(barrier, inc=1, device_id={"ctx": behind}, device_id_type=MESH)
    pl.semaphore_wait(barrier, tp + 1)

    incoming = (
        (k_in, kx, HEAD, halo_blocks),
        (v_in, vx, HEAD, halo_blocks),
        (q_in, qs, wide, 0),
        (g_in, gs, wide, 0),
    )

    def in_copy(i, owner, peer):
        source, target, width, first = incoming[i]
        return pltpu.make_async_remote_copy(
            src_ref=source.at[:, columns(peer, width)],
            dst_ref=target.at[at(first + owner), :],
            send_sem=in_send.at[i, peer],
            recv_sem=in_recv.at[i, owner],
            device_id={"tp": peer},
            device_id_type=MESH,
        )

    def own_copy(i):
        source, target, width, first = incoming[i]
        return pltpu.make_async_copy(
            source.at[:, columns(me, width)], target.at[at(first + me), :], own_in.at[i]
        )

    for i in range(4):
        def send(n, _, i=i):
            in_copy(i, me, lax.rem(me + n, tp)).start()
            return 0
        lax.fori_loop(1, tp, send, 0)
        own_copy(i).start()

    def arrived(i):
        def wait(n, _):
            in_copy(i, lax.rem(me + n, tp), me).wait_recv()
            return 0
        lax.fori_loop(1, tp, wait, 0)
        own_copy(i).wait()

    acc_k[...] = jnp.zeros_like(acc_k)
    acc_v[...] = jnp.zeros_like(acc_v)

    def halo_copy(i, source, target, where):
        return pltpu.make_async_remote_copy(
            src_ref=source, dst_ref=target, send_sem=halo_send.at[i], recv_sem=halo_recv.at[i],
            device_id={"ctx": where}, device_id_type=MESH,
        )

    halo_k = halo_copy(0, kx.at[pl.ds(shard, WINDOW), :], kx.at[pl.ds(0, WINDOW), :], ahead)
    halo_v = halo_copy(1, vx.at[pl.ds(shard, WINDOW), :], vx.at[pl.ds(0, WINDOW), :], ahead)
    halo_dk = halo_copy(2, halo_out.at[0], halo_in.at[0], behind)
    halo_dv = halo_copy(3, halo_out.at[1], halo_in.at[1], behind)

    def turn(source, target, first, count):
        def step(n, _):
            target[:, at(first + n)] = source[at(first + n), :].T
            return 0
        lax.fori_loop(0, count, step, 0)

    arrived(0)
    halo_k.start()
    turn(kx, kt, halo_blocks, blocks)
    arrived(1)
    halo_v.start()
    turn(vx, vt, halo_blocks, blocks)
    arrived(2)

    row_of = lax.broadcasted_iota(jnp.int32, (rows, wide), 0)
    col_of = lax.rem(lax.broadcasted_iota(jnp.int32, (rows, wide), 1), rows)
    causal = row_of <= col_of

    outgoing = (
        (o_buf, o_out, wide), (dq_buf, dq_out, wide), (dk_buf, dk_out, HEAD), (dv_buf, dv_out, HEAD),
    )

    def out_copy(i, owner, peer):
        source, target, width = outgoing[i]
        return pltpu.make_async_remote_copy(
            src_ref=source.at[peer],
            dst_ref=target.at[:, columns(owner, width)],
            send_sem=out_send.at[i, peer],
            recv_sem=out_recv.at[i, owner],
            device_id={"tp": peer},
            device_id_type=MESH,
        )

    def keep_copy(i):
        source, target, width = outgoing[i]
        return pltpu.make_async_copy(source.at[me], target.at[:, columns(me, width)], own_out.at[i])

    def deliver(i, b):
        @pl.when(b != me)
        def _():
            out_copy(i, me, b).start()

        @pl.when(b == me)
        def _():
            keep_copy(i).start()

    def stacked(ref, b):
        block = ref[at(b), :]
        return jnp.concatenate([block[:, :HEAD], block[:, HEAD:]], axis=0)

    def unstacked(t):
        return jnp.concatenate([t[:, :rows].T, t[:, rows:].T], axis=1)

    def fold(op, x):
        return op(x.reshape(rows // 8, 8, wide), axis=0)

    nt = (((1,), (1,)), ((), ()))
    chunks = WINDOW // rows

    def forward(b):
        query = stacked(qs, b)
        scores[...] = lax.dot_general(kx[at(b, span), :], query, nt, preferred_element_type=F32)
        present = [jnp.logical_or(place > 0, j + b >= halo_blocks) for j in range(chunks)]
        diagonal = scores[pl.ds(WINDOW, rows), :]
        scores[pl.ds(0, rows), :] = jnp.where(
            causal, diagonal, jnp.where(present[0], scores[pl.ds(0, rows), :], -FAR)
        )
        top = fold(jnp.max, scores[pl.ds(0, rows), :])
        for j in range(1, chunks):
            part = fold(jnp.max, scores[pl.ds(j * rows, rows), :])
            top = jnp.maximum(top, jnp.where(present[j], part, -FAR))
        shift = jnp.max(top, axis=0, keepdims=True) * EXP_SCALE
        total = jnp.zeros((8, wide), F32)
        for j in range(chunks):
            by = shift if j == 0 else jnp.where(present[j], shift, FAR)
            e = jnp.exp2(scores[pl.ds(j * rows, rows), :] * EXP_SCALE - by)
            total = total + fold(jnp.sum, e)
            if j == 0:
                ex[b, pl.ds(0, rows), :] = jnp.where(causal, 0.0, e).astype(BF16)
                ex[b, pl.ds(WINDOW, rows), :] = jnp.where(causal, e, 0.0).astype(BF16)
            else:
                ex[b, pl.ds(j * rows, rows), :] = e.astype(BF16)
        inverse = 1.0 / jnp.sum(total, axis=0, keepdims=True)
        rl[b] = inverse
        out = jnp.dot(vt[:, at(b, span)], ex[b], preferred_element_type=F32) * inverse
        out = out.astype(BF16)
        ot[b] = out
        o_buf[b] = unstacked(out)
        deliver(0, b)

    def backward(b):
        query = stacked(qs, b)
        grad_t = (stacked(gs, b).astype(F32).T * rl[b]).astype(BF16)
        delta = jnp.sum(grad_t.astype(F32) * ot[b].astype(F32), axis=0, keepdims=True)
        grad = grad_t.T
        scores[...] = jnp.dot(vx[at(b, span), :], grad_t, preferred_element_type=F32)
        first = jnp.where(causal, scores[pl.ds(WINDOW, rows), :], scores[pl.ds(0, rows), :])
        e = ex[b, pl.ds(0, rows), :].astype(F32) + ex[b, pl.ds(WINDOW, rows), :].astype(F32)
        d = e * (first - delta)
        dlog[pl.ds(0, rows), :] = jnp.where(causal, 0.0, d).astype(BF16)
        dlog[pl.ds(WINDOW, rows), :] = jnp.where(causal, d, 0.0).astype(BF16)
        for j in range(1, chunks):
            part = pl.ds(j * rows, rows)
            dlog[part, :] = (ex[b, part, :].astype(F32) * (scores[part, :] - delta)).astype(BF16)
        window = at(b, span)
        acc_v[window, :] += jnp.dot(ex[b], grad, preferred_element_type=F32)
        acc_k[window, :] += jnp.dot(dlog[...], query, preferred_element_type=F32)
        dq_t = jnp.dot(kt[:, window], dlog[...], preferred_element_type=F32) * SCALE
        dq_buf[b] = unstacked(dq_t.astype(BF16))
        deliver(1, b)

    half = blocks // 2

    def over(base, work):
        def step(n, _):
            work(base + lax.rem(n + me, half))
            return 0
        lax.fori_loop(0, half, step, 0)

    over(half, forward)
    halo_k.wait_recv()
    turn(kx, kt, 0, halo_blocks)
    halo_v.wait_recv()
    turn(vx, vt, 0, halo_blocks)
    over(0, forward)

    arrived(3)
    over(0, backward)

    def pack(n, _):
        halo_out[0, at(n), :] = (acc_k[at(n), :] * SCALE).astype(BF16)
        halo_out[1, at(n), :] = acc_v[at(n), :].astype(BF16)
        return 0
    lax.fori_loop(0, halo_blocks, pack, 0)
    halo_dk.start()
    halo_dv.start()
    over(half, backward)

    def finish_early(b):
        dk_buf[b] = (acc_k[at(b + halo_blocks), :] * SCALE).astype(BF16)
        dv_buf[b] = acc_v[at(b + halo_blocks), :].astype(BF16)
        deliver(2, b)
        deliver(3, b)

    def finish_late(b):
        more = at(b - (blocks - halo_blocks))
        dk_buf[b] = (acc_k[at(b + halo_blocks), :] * SCALE + halo_in[0, more, :].astype(F32)).astype(BF16)
        dv_buf[b] = (acc_v[at(b + halo_blocks), :] + halo_in[1, more, :].astype(F32)).astype(BF16)
        deliver(2, b)
        deliver(3, b)

    over(0, finish_early)
    halo_dk.wait_recv()
    halo_dv.wait_recv()
    over(half, finish_late)

    for i in range(4):
        def wait(n, _, i=i):
            peer = lax.rem(me + n, tp)
            in_copy(i, me, peer).wait_send()
            out_copy(i, me, peer).wait_send()
            out_copy(i, peer, me).wait_recv()
            return 0
        lax.fori_loop(1, tp, wait, 0)
        keep_copy(i).wait()
    for copy in (halo_k, halo_v, halo_dk, halo_dv):
        copy.wait_send()


def solution(mesh):
    tp, ctx = mesh.shape["tp"], mesh.shape["ctx"]

    def on_device(queries, keys, values, output_gradient):
        rows = queries.shape[0]
        shard = rows * tp
        wide = GROUP * HEAD
        span = WINDOW + rows
        hbm = pl.BlockSpec(memory_space=pl.ANY)
        dma = pltpu.SemaphoreType.DMA
        return pl.pallas_call(
            functools.partial(attention_kernel, tp, ctx, rows),
            out_shape=[
                jax.ShapeDtypeStruct(queries.shape, BF16),
                jax.ShapeDtypeStruct(queries.shape, BF16),
                jax.ShapeDtypeStruct(keys.shape, BF16),
                jax.ShapeDtypeStruct(keys.shape, BF16),
            ],
            in_specs=[hbm] * 4,
            out_specs=[hbm] * 4,
            scratch_shapes=[
                pltpu.VMEM((shard, wide), BF16),
                pltpu.VMEM((WINDOW + shard, HEAD), BF16),
                pltpu.VMEM((WINDOW + shard, HEAD), BF16),
                pltpu.VMEM((shard, wide), BF16),
                pltpu.VMEM((HEAD, WINDOW + shard), BF16),
                pltpu.VMEM((HEAD, WINDOW + shard), BF16),
                pltpu.VMEM((span, wide), F32),
                pltpu.VMEM((tp, span, wide), BF16),
                pltpu.VMEM((tp, HEAD, wide), BF16),
                pltpu.VMEM((tp, 1, wide), F32),
                pltpu.VMEM((WINDOW + shard, HEAD), F32),
                pltpu.VMEM((WINDOW + shard, HEAD), F32),
                pltpu.VMEM((span, wide), BF16),
                pltpu.VMEM((tp, rows, wide), BF16),
                pltpu.VMEM((tp, rows, wide), BF16),
                pltpu.VMEM((tp, rows, HEAD), BF16),
                pltpu.VMEM((tp, rows, HEAD), BF16),
                pltpu.VMEM((2, WINDOW, HEAD), BF16),
                pltpu.VMEM((2, WINDOW, HEAD), BF16),
                dma((4, tp)), dma((4, tp)), dma((4, tp)), dma((4, tp)),
                dma((4,)), dma((4,)), dma((4,)), dma((4,)),
            ],
            compiler_params=pltpu.CompilerParams(
                collective_id=0, has_side_effects=True, vmem_limit_bytes=60 << 20
            ),
        )(queries, keys, values, output_gradient)

    spec = P(("ctx", "tp"), None)
    return jax.shard_map(
        on_device, mesh=mesh, in_specs=(spec,) * 4, out_specs=(spec,) * 4, check_vma=False
    )
```

profile of v0, /device:TPU:112, one launch (start us, length us, event | category | flops | bytes accessed | tf_op | source)
XLA Modules:
  0.0 93.3 jit_solution(14053261612206030781)
XLA Ops:
  0.6 86.8 %shard_map.75 = (bf16[128,4096]{1,0:T(8,128)(2,1)}, bf16[128,4096]{1,0:T(8,128)(2,1)}, bf16[128,2048]{1,0:T(8,128)(2,1)}, bf16[128,2048]{1,0:T(8,128)(2,1)}) custom-call(bf16[128,4096]{1,0:T(8,128)(2,1)} %q_in.1, bf16[128,2048]{1,0:T(8,128)(2,1)} %k_in.1, bf16[128,2048]{1,0:T(8,128)(2,1)} %v_in.1, bf16[128,4096]{1,0:T(8,128)(2,1)} %g_in.1), custom_call_target="tpu_custom_call" | custom-call | tf_op jit(solution)/shard_map/pallas_call | solution.py:284
  87.4 0.0 copy-start
  87.5 2.4 %copy.12 = bf16[128,4096]{1,0:T(8,128)(2,1)} copy(bf16[128,4096]{1,0:T(8,128)(2,1)} %get-tuple-element.8) | data formatting | bytes 2097152
  89.8 0.0 copy-done
  89.8 0.0 copy-start.2
  89.8 1.0 %copy.13 = bf16[128,4096]{1,0:T(8,128)(2,1)} copy(bf16[128,4096]{1,0:T(8,128)(2,1)S(1)} %copy-done) | data formatting | bytes 2097152
  90.8 0.4 copy-done.2
  91.2 0.0 copy-start.1
  91.2 0.8 copy.14
  92.0 0.4 copy-done.1
  92.5 0.8 copy.15
Async XLA Ops:
  87.4 2.4 %copy-start = (bf16[128,4096]{1,0:T(8,128)(2,1)S(1)}, bf16[128,4096]{1,0:T(8,128)(2,1)}, u32[]{:S(2)}) copy-start(bf16[128,4096]{1,0:T(8,128)(2,1)} %get-tuple-element.9) | copy-start | bytes 3145732
  89.8 1.4 %copy-start.2 = (bf16[128,2048]{1,0:T(8,128)(2,1)S(1)}, bf16[128,2048]{1,0:T(8,128)(2,1)}, u32[]{:S(2)}) copy-start(bf16[128,2048]{1,0:T(8,128)(2,1)} %get-tuple-element.10) | copy-start | bytes 1572868
  91.2 1.2 %copy-start.1 = (bf16[128,2048]{1,0:T(8,128)(2,1)S(1)}, bf16[128,2048]{1,0:T(8,128)(2,1)}, u32[]{:S(2)}) copy-start(bf16[128,2048]{1,0:T(8,128)(2,1)} %get-tuple-element.11) | copy-start | bytes 1572868
where the time goes:
time: 95.1 us; the launch traced here: 93.3 us
  Pallas kernels  86.8 us (91%)
  local copies, waits for them, and re-layouts  5.8 us (6%)
    pallas_call x1, Pallas kernels, on_device(): pl.pallas_call(functools.partial(attention_kernel, tp, ctx, rows), out_sh...  86.8 us
    unnamed x10, local copies, waits for them, and re-layouts  5.8 us

commit v1 on v0

--- a/solution.py
+++ b/solution.py
@@ -15,6 +15,7 @@
 SCALE = QSCALE ** (-0.5)
 EXP_SCALE = SCALE * math.log2(math.e)
 FAR = 1e30
+FIRST = (0, 1, 2)
 MESH = pl.DeviceIdType.MESH
 F32 = jnp.float32
 BF16 = jnp.bfloat16
@@ -74,11 +75,32 @@
             source.at[:, columns(me, width)], target.at[at(first + me), :], own_in.at[i]
         )
 
+    side = math.isqrt(tp)
+    x, y = lax.rem(me, side), me // side
+    core = lax.rem(place, 2)
+
+    def partner(dx, dy):
+        dx = jnp.where(core == 0, dx, side - dx)
+        dy = jnp.where(core == 0, dy, side - dy)
+        return lax.rem(y + dy, side) * side + lax.rem(x + dx, side)
+
+    far = sorted(
+        ((dx, dy) for dx in range(side) for dy in range(side) if dx or dy),
+        key=lambda d: -(min(d[0], side - d[0]) + min(d[1], side - d[1])),
+    )
+    partners = [partner(dx, dy) for dx, dy in far]
+
+    def send(i):
+        for peer in partners:
+            in_copy(i, me, peer).start()
+
+    def sent(i):
+        for peer in partners:
+            in_copy(i, me, peer).wait_send()
+
+    for i in FIRST:
+        send(i)
     for i in range(4):
-        def send(n, _, i=i):
-            in_copy(i, me, lax.rem(me + n, tp)).start()
-            return 0
-        lax.fori_loop(1, tp, send, 0)
         own_copy(i).start()
 
     def arrived(i):
@@ -114,6 +136,15 @@
     arrived(1)
     halo_v.start()
     turn(vx, vt, halo_blocks, blocks)
+    for i in FIRST:
+        sent(i)
+    for i in range(4):
+        if i not in FIRST:
+            send(i)
+    halo_k.wait_recv()
+    turn(kx, kt, 0, halo_blocks)
+    halo_v.wait_recv()
+    turn(vx, vt, 0, halo_blocks)
     arrived(2)
 
     row_of = lax.broadcasted_iota(jnp.int32, (rows, wide), 0)
@@ -215,21 +246,20 @@
 
     half = blocks // 2
 
-    def over(base, work):
+    def over(base, count, work):
         def step(n, _):
-            work(base + lax.rem(n + me, half))
+            high = count // side
+            dx = lax.rem(2 + lax.rem(n, side), side)
+            dy = lax.rem(high // 2 + n // side, high)
+            bx = lax.rem(x + jnp.where(core == 0, dx, side - dx), side)
+            by = lax.rem(y + jnp.where(core == 0, dy, high - dy), high)
+            work(base + by * side + bx)
             return 0
-        lax.fori_loop(0, half, step, 0)
-
-    over(half, forward)
-    halo_k.wait_recv()
-    turn(kx, kt, 0, halo_blocks)
-    halo_v.wait_recv()
-    turn(vx, vt, 0, halo_blocks)
-    over(0, forward)
-
+        lax.fori_loop(0, count, step, 0)
+
+    over(0, blocks, forward)
     arrived(3)
-    over(0, backward)
+    over(0, half, backward)
 
     def pack(n, _):
         halo_out[0, at(n), :] = (acc_k[at(n), :] * SCALE).astype(BF16)
@@ -238,35 +268,34 @@
     lax.fori_loop(0, halo_blocks, pack, 0)
     halo_dk.start()
     halo_dv.start()
-    over(half, backward)
-
-    def finish_early(b):
-        dk_buf[b] = (acc_k[at(b + halo_blocks), :] * SCALE).astype(BF16)
-        dv_buf[b] = acc_v[at(b + halo_blocks), :].astype(BF16)
-        deliver(2, b)
-        deliver(3, b)
-
-    def finish_late(b):
-        more = at(b - (blocks - halo_blocks))
-        dk_buf[b] = (acc_k[at(b + halo_blocks), :] * SCALE + halo_in[0, more, :].astype(F32)).astype(BF16)
-        dv_buf[b] = (acc_v[at(b + halo_blocks), :] + halo_in[1, more, :].astype(F32)).astype(BF16)
-        deliver(2, b)
-        deliver(3, b)
-
-    over(0, finish_early)
+    over(half, half, backward)
+
     halo_dk.wait_recv()
     halo_dv.wait_recv()
-    over(half, finish_late)
+
+    def finish(b):
+        late = b - (blocks - halo_blocks)
+        more = at(jnp.maximum(late, 0))
+        weight = (late >= 0).astype(F32)
+        own = at(b + halo_blocks)
+        dk_buf[b] = (acc_k[own, :] * SCALE + weight * halo_in[0, more, :].astype(F32)).astype(BF16)
+        deliver(2, b)
+        dv_buf[b] = (acc_v[own, :] + weight * halo_in[1, more, :].astype(F32)).astype(BF16)
+        deliver(3, b)
+
+    over(0, blocks, finish)
 
     for i in range(4):
         def wait(n, _, i=i):
             peer = lax.rem(me + n, tp)
-            in_copy(i, me, peer).wait_send()
             out_copy(i, me, peer).wait_send()
             out_copy(i, peer, me).wait_recv()
             return 0
         lax.fori_loop(1, tp, wait, 0)
         keep_copy(i).wait()
+    for i in range(4):
+        if i not in FIRST:
+            sent(i)
     for copy in (halo_k, halo_v, halo_dk, halo_dv):
         copy.wait_send()
 
@@ -280,17 +309,13 @@
         wide = GROUP * HEAD
         span = WINDOW + rows
         hbm = pl.BlockSpec(memory_space=pl.ANY)
+        vmem = pl.BlockSpec(memory_space=pltpu.VMEM)
         dma = pltpu.SemaphoreType.DMA
-        return pl.pallas_call(
+        results = pl.pallas_call(
             functools.partial(attention_kernel, tp, ctx, rows),
-            out_shape=[
-                jax.ShapeDtypeStruct(queries.shape, BF16),
-                jax.ShapeDtypeStruct(queries.shape, BF16),
-                jax.ShapeDtypeStruct(keys.shape, BF16),
-                jax.ShapeDtypeStruct(keys.shape, BF16),
-            ],
+            out_shape=[pltpu.VMEM(a.shape, BF16) for a in (queries, queries, keys, keys)],
             in_specs=[hbm] * 4,
-            out_specs=[hbm] * 4,
+            out_specs=[vmem] * 4,
             scratch_shapes=[
                 pltpu.VMEM((shard, wide), BF16),
                 pltpu.VMEM((WINDOW + shard, HEAD), BF16),
@@ -318,6 +343,7 @@
                 collective_id=0, has_side_effects=True, vmem_limit_bytes=60 << 20
             ),
         )(queries, keys, values, output_gradient)
+        return results
 
     spec = P(("ctx", "tp"), None)
     return jax.shard_map(

time: 95.1 us -> 88.1 us (0.926)
  the two profiles are of different devices: /device:TPU:112 before, /device:TPU:65 now
where the time goes in v1:
time: 88.1 us
  Pallas kernels  83.9 us (95%)
  local copies, waits for them, and re-layouts  3.53 us (4%)
    pallas_call x1, Pallas kernels, on_device(): pl.pallas_call(functools.partial(attention_kernel, tp, ctx, rows), out_sh...  83.9 us
    unnamed x4, local copies, waits for them, and re-layouts  3.53 us

profile of v1, /device:TPU:65, one launch (start us, length us, event | category | flops | bytes accessed | tf_op | source)
XLA Modules:
  0.0 88.1 jit_solution(2757057162418823027)
XLA Ops:
  0.6 83.9 %shard_map.75 = (bf16[128,4096]{1,0:T(8,128)(2,1)S(1)}, bf16[128,4096]{1,0:T(8,128)(2,1)S(1)}, bf16[128,2048]{1,0:T(8,128)(2,1)S(1)}, bf16[128,2048]{1,0:T(8,128)(2,1)S(1)}) custom-call(bf16[128,4096]{1,0:T(8,128)(2,1)} %q_in.1, bf16[128,2048]{1,0:T(8,128)(2,1)} %k_in.1, bf16[128,2048]{1,0:T(8,128)(2,1)} %v_in.1, bf16[128,4096]{1,0:T(8,128)(2,1)} %g_in.1), custom_call_target="tpu_custom_call" | custom-call | tf_op jit(solution)/shard_map/pallas_call | solution.py:314
  84.5 1.0 %copy.12 = bf16[128,4096]{1,0:T(8,128)(2,1)} copy(bf16[128,4096]{1,0:T(8,128)(2,1)S(1)} %get-tuple-element.4) | data formatting | bytes 2097152
  85.5 0.8 copy.14
  86.3 0.8 copy.15
  87.1 1.0 %copy.13 = bf16[128,4096]{1,0:T(8,128)(2,1)} copy(bf16[128,4096]{1,0:T(8,128)(2,1)S(1)} %get-tuple-element.5) | data formatting | bytes 2097152

commit v2 on v1

--- a/solution.py
+++ b/solution.py
@@ -16,6 +16,7 @@
 EXP_SCALE = SCALE * math.log2(math.e)
 FAR = 1e30
 FIRST = (0, 1, 2)
+EARLY = 10
 MESH = pl.DeviceIdType.MESH
 F32 = jnp.float32
 BF16 = jnp.bfloat16
@@ -25,7 +26,7 @@
     tp, ctx, rows,
     q_in, k_in, v_in, g_in,
     o_out, dq_out, dk_out, dv_out,
-    qs, kx, vx, gs, kt, vt, scores, ex, ot, rl, acc_k, acc_v, dlog,
+    qs, kx, vx, gs, kt, vt, scores, scores_too, ex, ot, rl, acc_k, acc_v, dlog,
     o_buf, dq_buf, dk_buf, dv_buf, halo_out, halo_in,
     in_send, in_recv, out_send, out_recv, halo_send, halo_recv, own_in, own_out,
 ):
@@ -90,6 +91,12 @@
     )
     partners = [partner(dx, dy) for dx, dy in far]
 
+    def nth_partner(n):
+        peer = partners[0]
+        for i in range(1, tp - 1):
+            peer = jnp.where(n == i, partners[i], peer)
+        return peer
+
     def send(i):
         for peer in partners:
             in_copy(i, me, peer).start()
@@ -110,6 +117,15 @@
         lax.fori_loop(1, tp, wait, 0)
         own_copy(i).wait()
 
+    def arrived_block(i, b):
+        @pl.when(b != me)
+        def _():
+            in_copy(i, b, me).wait_recv()
+
+        @pl.when(b == me)
+        def _():
+            own_copy(i).wait()
+
     acc_k[...] = jnp.zeros_like(acc_k)
     acc_v[...] = jnp.zeros_like(acc_v)
 
@@ -126,26 +142,26 @@
 
     def turn(source, target, first, count):
         def step(n, _):
-            target[:, at(first + n)] = source[at(first + n), :].T
+            part = at(first + 4 * n, 4 * rows)
+            target[:, part] = source[part, :].T
             return 0
-        lax.fori_loop(0, count, step, 0)
+        lax.fori_loop(0, count // 4, step, 0)
 
     arrived(0)
     halo_k.start()
-    turn(kx, kt, halo_blocks, blocks)
     arrived(1)
     halo_v.start()
+    turn(kx, kt, halo_blocks, blocks)
     turn(vx, vt, halo_blocks, blocks)
-    for i in FIRST:
-        sent(i)
-    for i in range(4):
-        if i not in FIRST:
-            send(i)
+    sent(0)
+    sent(1)
+    for peer in partners[:EARLY]:
+        in_copy(2, me, peer).wait_send()
+    send(3)
     halo_k.wait_recv()
     turn(kx, kt, 0, halo_blocks)
     halo_v.wait_recv()
     turn(vx, vt, 0, halo_blocks)
-    arrived(2)
 
     row_of = lax.broadcasted_iota(jnp.int32, (rows, wide), 0)
     col_of = lax.rem(lax.broadcasted_iota(jnp.int32, (rows, wide), 1), rows)
@@ -192,7 +208,7 @@
     nt = (((1,), (1,)), ((), ()))
     chunks = WINDOW // rows
 
-    def forward(b):
+    def forward(b, scores):
         query = stacked(qs, b)
         scores[...] = lax.dot_general(kx[at(b, span), :], query, nt, preferred_element_type=F32)
         present = [jnp.logical_or(place > 0, j + b >= halo_blocks) for j in range(chunks)]
@@ -221,9 +237,9 @@
         out = out.astype(BF16)
         ot[b] = out
         o_buf[b] = unstacked(out)
-        deliver(0, b)
 
     def backward(b):
+        arrived_block(3, b)
         query = stacked(qs, b)
         grad_t = (stacked(gs, b).astype(F32).T * rl[b]).astype(BF16)
         delta = jnp.sum(grad_t.astype(F32) * ot[b].astype(F32), axis=0, keepdims=True)
@@ -257,8 +273,17 @@
             return 0
         lax.fori_loop(0, count, step, 0)
 
-    over(0, blocks, forward)
-    arrived(3)
+    def front(n, _):
+        pair = (nth_partner(2 * n), jnp.where(n == tp // 2 - 1, me, nth_partner(2 * n + 1)))
+        for b in pair:
+            arrived_block(2, b)
+        forward(pair[0], scores)
+        forward(pair[1], scores_too)
+        for b in pair:
+            deliver(0, b)
+        return 0
+
+    lax.fori_loop(0, tp // 2, front, 0)
     over(0, half, backward)
 
     def pack(n, _):
@@ -270,20 +295,22 @@
     halo_dv.start()
     over(half, half, backward)
 
+    def finish(b, late):
+        own = at(b + halo_blocks)
+        dk, dv = acc_k[own, :] * SCALE, acc_v[own, :]
+        if late:
+            more = at(b - (blocks - halo_blocks))
+            dk += halo_in[0, more, :].astype(F32)
+            dv += halo_in[1, more, :].astype(F32)
+        dk_buf[b] = dk.astype(BF16)
+        deliver(2, b)
+        dv_buf[b] = dv.astype(BF16)
+        deliver(3, b)
+
+    over(0, half, functools.partial(finish, late=False))
     halo_dk.wait_recv()
     halo_dv.wait_recv()
-
-    def finish(b):
-        late = b - (blocks - halo_blocks)
-        more = at(jnp.maximum(late, 0))
-        weight = (late >= 0).astype(F32)
-        own = at(b + halo_blocks)
-        dk_buf[b] = (acc_k[own, :] * SCALE + weight * halo_in[0, more, :].astype(F32)).astype(BF16)
-        deliver(2, b)
-        dv_buf[b] = (acc_v[own, :] + weight * halo_in[1, more, :].astype(F32)).astype(BF16)
-        deliver(3, b)
-
-    over(0, blocks, finish)
+    over(half, half, functools.partial(finish, late=True))
 
     for i in range(4):
         def wait(n, _, i=i):
@@ -293,9 +320,9 @@
             return 0
         lax.fori_loop(1, tp, wait, 0)
         keep_copy(i).wait()
-    for i in range(4):
-        if i not in FIRST:
-            sent(i)
+    for peer in partners[EARLY:]:
+        in_copy(2, me, peer).wait_send()
+    sent(3)
     for copy in (halo_k, halo_v, halo_dk, halo_dv):
         copy.wait_send()
 
@@ -324,6 +351,7 @@
                 pltpu.VMEM((HEAD, WINDOW + shard), BF16),
                 pltpu.VMEM((HEAD, WINDOW + shard), BF16),
                 pltpu.VMEM((span, wide), F32),
+                pltpu.VMEM((span, wide), F32),
                 pltpu.VMEM((tp, span, wide), BF16),
                 pltpu.VMEM((tp, HEAD, wide), BF16),
                 pltpu.VMEM((tp, 1, wide), F32),

time: 88.1 us -> 87.7 us (level)
  the two profiles are of different devices: /device:TPU:65 before, /device:TPU:112 now
where the time goes in v2:
time: 87.7 us; the launch traced here: 87.6 us
  Pallas kernels  83.4 us (95%)
  local copies, waits for them, and re-layouts  3.53 us (4%)
    pallas_call x1, Pallas kernels, on_device(): pl.pallas_call(functools.partial(attention_kernel, tp, ctx, rows), out_sh...  83.4 us
    unnamed x4, local copies, waits for them, and re-layouts  3.53 us

profile of v2, /device:TPU:112, one launch (start us, length us, event | category | flops | bytes accessed | tf_op | source)
XLA Modules:
  0.0 87.6 jit_solution(13570227558803839581)
XLA Ops:
  0.6 83.4 %shard_map.75 = (bf16[128,4096]{1,0:T(8,128)(2,1)S(1)}, bf16[128,4096]{1,0:T(8,128)(2,1)S(1)}, bf16[128,2048]{1,0:T(8,128)(2,1)S(1)}, bf16[128,2048]{1,0:T(8,128)(2,1)S(1)}) custom-call(bf16[128,4096]{1,0:T(8,128)(2,1)} %q_in.1, bf16[128,2048]{1,0:T(8,128)(2,1)} %k_in.1, bf16[128,2048]{1,0:T(8,128)(2,1)} %v_in.1, bf16[128,4096]{1,0:T(8,128)(2,1)} %g_in.1), custom_call_target="tpu_custom_call" | custom-call | tf_op jit(solution)/shard_map/pallas_call | solution.py:341
  84.1 1.0 %copy.12 = bf16[128,4096]{1,0:T(8,128)(2,1)} copy(bf16[128,4096]{1,0:T(8,128)(2,1)S(1)} %get-tuple-element.4) | data formatting | bytes 2097152
  85.1 0.8 copy.14
  85.8 0.8 copy.15
  86.6 1.0 %copy.13 = bf16[128,4096]{1,0:T(8,128)(2,1)} copy(bf16[128,4096]{1,0:T(8,128)(2,1)S(1)} %get-tuple-element.5) | data formatting | bytes 2097152

commit v3 on v2

--- a/solution.py
+++ b/solution.py
@@ -26,7 +26,7 @@
     tp, ctx, rows,
     q_in, k_in, v_in, g_in,
     o_out, dq_out, dk_out, dv_out,
-    qs, kx, vx, gs, kt, vt, scores, scores_too, ex, ot, rl, acc_k, acc_v, dlog,
+    qs, kx, vx, gs, kt, vt, scores, scores_too, ex, ot, rl, acc_k, acc_v, dlog, dlog_too,
     o_buf, dq_buf, dk_buf, dv_buf, halo_out, halo_in,
     in_send, in_recv, out_send, out_recv, halo_send, halo_recv, own_in, own_out,
 ):
@@ -238,8 +238,7 @@
         ot[b] = out
         o_buf[b] = unstacked(out)
 
-    def backward(b):
-        arrived_block(3, b)
+    def backward(b, scores, dlog):
         query = stacked(qs, b)
         grad_t = (stacked(gs, b).astype(F32).T * rl[b]).astype(BF16)
         delta = jnp.sum(grad_t.astype(F32) * ot[b].astype(F32), axis=0, keepdims=True)
@@ -258,20 +257,30 @@
         acc_k[window, :] += jnp.dot(dlog[...], query, preferred_element_type=F32)
         dq_t = jnp.dot(kt[:, window], dlog[...], preferred_element_type=F32) * SCALE
         dq_buf[b] = unstacked(dq_t.astype(BF16))
-        deliver(1, b)
 
     half = blocks // 2
 
-    def over(base, count, work):
-        def step(n, _):
+    def over(base, count, work, many=1):
+        def place_of(n):
             high = count // side
             dx = lax.rem(2 + lax.rem(n, side), side)
             dy = lax.rem(high // 2 + n // side, high)
             bx = lax.rem(x + jnp.where(core == 0, dx, side - dx), side)
             by = lax.rem(y + jnp.where(core == 0, dy, high - dy), high)
-            work(base + by * side + bx)
+            return base + by * side + bx
+
+        def step(n, _):
+            work(*[place_of(many * n + i) for i in range(many)])
             return 0
-        lax.fori_loop(0, count, step, 0)
+        lax.fori_loop(0, count // many, step, 0)
+
+    def back(*pair):
+        for b in pair:
+            arrived_block(3, b)
+        backward(pair[0], scores, dlog)
+        backward(pair[1], scores_too, dlog_too)
+        for b in pair:
+            deliver(1, b)
 
     def front(n, _):
         pair = (nth_partner(2 * n), jnp.where(n == tp // 2 - 1, me, nth_partner(2 * n + 1)))
@@ -284,7 +293,7 @@
         return 0
 
     lax.fori_loop(0, tp // 2, front, 0)
-    over(0, half, backward)
+    over(0, half, back, 2)
 
     def pack(n, _):
         halo_out[0, at(n), :] = (acc_k[at(n), :] * SCALE).astype(BF16)
@@ -293,7 +302,7 @@
     lax.fori_loop(0, halo_blocks, pack, 0)
     halo_dk.start()
     halo_dv.start()
-    over(half, half, backward)
+    over(half, half, back, 2)
 
     def finish(b, late):
         own = at(b + halo_blocks)
@@ -358,6 +367,7 @@
                 pltpu.VMEM((WINDOW + shard, HEAD), F32),
                 pltpu.VMEM((WINDOW + shard, HEAD), F32),
                 pltpu.VMEM((span, wide), BF16),
+                pltpu.VMEM((span, wide), BF16),
                 pltpu.VMEM((tp, rows, wide), BF16),
                 pltpu.VMEM((tp, rows, wide), BF16),
                 pltpu.VMEM((tp, rows, HEAD), BF16),

time: 87.7 us -> 87.7 us (level)
  no operation moved by 1% of the time
where the time goes in v3:
time: 87.7 us; the launch traced here: 87.6 us
  Pallas kernels  83.4 us (95%)
  local copies, waits for them, and re-layouts  3.53 us (4%)
    pallas_call x1, Pallas kernels, on_device(): pl.pallas_call(functools.partial(attention_kernel, tp, ctx, rows), out_sh...  83.4 us
    unnamed x4, local copies, waits for them, and re-layouts  3.53 us

profile of v3, /device:TPU:112, one launch (start us, length us, event | category | flops | bytes accessed | tf_op | source)
XLA Modules:
  0.0 87.6 jit_solution(1775936568823823415)
XLA Ops:
  0.6 83.4 %shard_map.75 = (bf16[128,4096]{1,0:T(8,128)(2,1)S(1)}, bf16[128,4096]{1,0:T(8,128)(2,1)S(1)}, bf16[128,2048]{1,0:T(8,128)(2,1)S(1)}, bf16[128,2048]{1,0:T(8,128)(2,1)S(1)}) custom-call(bf16[128,4096]{1,0:T(8,128)(2,1)} %q_in.1, bf16[128,2048]{1,0:T(8,128)(2,1)} %k_in.1, bf16[128,2048]{1,0:T(8,128)(2,1)} %v_in.1, bf16[128,4096]{1,0:T(8,128)(2,1)} %g_in.1), custom_call_target="tpu_custom_call" | custom-call | tf_op jit(solution)/shard_map/pallas_call | solution.py:350
  84.1 1.0 %copy.12 = bf16[128,4096]{1,0:T(8,128)(2,1)} copy(bf16[128,4096]{1,0:T(8,128)(2,1)S(1)} %get-tuple-element.4) | data formatting | bytes 2097152
  85.1 0.8 copy.14
  85.9 0.8 copy.15
  86.6 1.0 %copy.13 = bf16[128,4096]{1,0:T(8,128)(2,1)} copy(bf16[128,4096]{1,0:T(8,128)(2,1)S(1)} %get-tuple-element.5) | data formatting | bytes 2097152

commit v4 on v2

--- a/solution.py
+++ b/solution.py
@@ -16,7 +16,7 @@
 EXP_SCALE = SCALE * math.log2(math.e)
 FAR = 1e30
 FIRST = (0, 1, 2)
-EARLY = 10
+EARLY = 7
 MESH = pl.DeviceIdType.MESH
 F32 = jnp.float32
 BF16 = jnp.bfloat16

time: 87.7 us -> 87.7 us (level)
  no operation moved by 1% of the time
where the time goes in v4:
time: 87.7 us; the launch traced here: 87.6 us
  Pallas kernels  83.4 us (95%)
  local copies, waits for them, and re-layouts  3.53 us (4%)
    pallas_call x1, Pallas kernels, on_device(): pl.pallas_call(functools.partial(attention_kernel, tp, ctx, rows), out_sh...  83.4 us
    unnamed x4, local copies, waits for them, and re-layouts  3.53 us

profile of v4, /device:TPU:112, one launch (start us, length us, event | category | flops | bytes accessed | tf_op | source)
XLA Modules:
  0.0 87.6 jit_solution(6829835126867656761)
XLA Ops:
  0.6 83.4 %shard_map.75 = (bf16[128,4096]{1,0:T(8,128)(2,1)S(1)}, bf16[128,4096]{1,0:T(8,128)(2,1)S(1)}, bf16[128,2048]{1,0:T(8,128)(2,1)S(1)}, bf16[128,2048]{1,0:T(8,128)(2,1)S(1)}) custom-call(bf16[128,4096]{1,0:T(8,128)(2,1)} %q_in.1, bf16[128,2048]{1,0:T(8,128)(2,1)} %k_in.1, bf16[128,2048]{1,0:T(8,128)(2,1)} %v_in.1, bf16[128,4096]{1,0:T(8,128)(2,1)} %g_in.1), custom_call_target="tpu_custom_call" | custom-call | tf_op jit(solution)/shard_map/pallas_call | solution.py:341
  84.1 1.0 %copy.12 = bf16[128,4096]{1,0:T(8,128)(2,1)} copy(bf16[128,4096]{1,0:T(8,128)(2,1)S(1)} %get-tuple-element.4) | data formatting | bytes 2097152
  85.1 0.8 copy.14
  85.9 0.8 copy.15
  86.6 1.0 %copy.13 = bf16[128,4096]{1,0:T(8,128)(2,1)} copy(bf16[128,4096]{1,0:T(8,128)(2,1)S(1)} %get-tuple-element.5) | data formatting | bytes 2097152
